TPU v7x, 256 devices: a whole 4x4x8 slice. The times are simulated.
256 devices in a mesh: row: 16 (over z, core), col: 16 (over x, y).
Axes of the slice: x: 4, y: 4, z: 8, core: 2. Of those that a mesh axis runs over, the one named last changes fastest.
Arguments:
- tokens: bfloat16 [4096, 8192], P('row', 'col'), may hold values from -6 to 6
- out_grad: bfloat16 [4096, 8192], P('row', 'col'), may hold values from -1.5 to 1.5
- gate_weight: bfloat16 [112, 1024, 128], P('col', 'row'), may hold values from -0.1875 to 0.1875
- up_weight: bfloat16 [112, 1024, 128], P('col', 'row'), may hold values from -0.1875 to 0.1875
- down_weight: bfloat16 [112, 1024, 128], P('col', 'row'), may hold values from -0.125 to 0.125
- gate_rows: int32 [112, 8], P('col'), may hold values from 0 to 63, all different within a row
- up_rows: int32 [112, 8], P('col'), may hold values from 0 to 63, all different within a row
- down_columns: int32 [112, 8], P('col'), may hold values from 0 to 63, all different within a row
Outputs:
- output: bfloat16 [4096, 8192], P('row', 'col')
- input_grad: bfloat16 [4096, 8192], P('row', 'col')
- gate_weight_grad: bfloat16 [112, 1024, 128], P('col', 'row')
- up_weight_grad: bfloat16 [112, 1024, 128], P('col', 'row')
- down_weight_grad: bfloat16 [112, 1024, 128], P('col', 'row')
Inputs may be any that keep to these rules, and one draw needn't show every extreme that they name: `gate_rows`: each row names 8 different block-rows; every block-row is named in some row. `up_rows`: each row names 8 different block-rows; every block-row is named in some row. `down_columns`: each row names 8 different output block-columns; every block-column is named in some row.
All inputs are finite; a program needn't handle non-finite values.
Results may differ from a plain program's by a relative error of at most 0.018.
Values may be sent and summed in bfloat16 or wider, within the bound.
A program may use at most 128 MiB of HBM per device.

v0:
```python
import jax
import jax.numpy as jnp
from jax import lax
from jax.sharding import PartitionSpec as P

D = 8192
BS = 128
KG = 8
KH = 8
DB = 64


def spread(contrib, block_lists):
    rows_here = contrib.shape[0]
    zero_block = jnp.zeros((rows_here, DB, BS), jnp.float32)
    placed = zero_block.at[:, block_lists.reshape(-1)].add(contrib.reshape(rows_here, -1, BS))
    return placed.reshape(rows_here, D)


def shards(tokens, out_grad, gate_weight, up_weight, down_weight, gate_rows, up_rows, down_columns):
    panels = lax.all_gather(jnp.stack([tokens, out_grad]), "col", axis=2, tiled=True)
    panel_in, panel_grad = (panels[0], panels[1])
    rows_here = panel_in.shape[0]
    owned_slots = gate_weight.shape[0]
    tiles = lax.all_gather(
        jnp.concatenate([gate_weight, up_weight, down_weight], axis=0), "row", axis=1, tiled=True
    )
    gate_tiles = tiles[:owned_slots]
    up_tiles = tiles[owned_slots : 2 * owned_slots]
    down_tiles = tiles[2 * owned_slots :]
    gate_four = gate_tiles.reshape(owned_slots, KG, BS, BS)
    up_four = up_tiles.reshape(owned_slots, KG, BS, BS)
    blocks_in = panel_in.reshape(rows_here, DB, BS)
    picked_gate = jnp.take(blocks_in, gate_rows.reshape(-1), axis=1).reshape(
        rows_here, owned_slots, KG, BS
    )
    picked_up = jnp.take(blocks_in, up_rows.reshape(-1), axis=1).reshape(
        rows_here, owned_slots, KG, BS
    )
    gate_value = jnp.einsum(
        "tfkr,fkri->tfi", picked_gate, gate_four, preferred_element_type=jnp.float32
    )
    up_value = jnp.einsum("tfkr,fkri->tfi", picked_up, up_four, preferred_element_type=jnp.float32)
    sigmoid_gate = jax.nn.sigmoid(gate_value)
    silu_gate = gate_value * sigmoid_gate
    hidden = (silu_gate * up_value).astype(jnp.bfloat16)
    down_four = down_tiles.reshape(owned_slots, KH, BS, BS)
    out_part = jnp.einsum("tfi,fkji->tfkj", hidden, down_four, preferred_element_type=jnp.float32)
    partial_out = spread(out_part, down_columns)
    blocks_grad = panel_grad.reshape(rows_here, DB, BS)
    picked_grad = jnp.take(blocks_grad, down_columns.reshape(-1), axis=1).reshape(
        rows_here, owned_slots, KH, BS
    )
    hidden_grad = jnp.einsum(
        "tfkj,fkji->tfi", picked_grad, down_four, preferred_element_type=jnp.float32
    )
    gate_grad = (
        hidden_grad * up_value * sigmoid_gate * (1.0 + gate_value * (1.0 - sigmoid_gate))
    ).astype(jnp.bfloat16)
    up_grad = (hidden_grad * silu_gate).astype(jnp.bfloat16)
    from_gate = jnp.einsum(
        "tfi,fkri->tfkr", gate_grad, gate_four, preferred_element_type=jnp.float32
    )
    from_up = jnp.einsum("tfi,fkri->tfkr", up_grad, up_four, preferred_element_type=jnp.float32)
    partial_in = spread(from_gate, gate_rows) + spread(from_up, up_rows)
    gate_partial = jnp.einsum(
        "tfkr,tfi->fkri", picked_gate, gate_grad, preferred_element_type=jnp.float32
    ).reshape(owned_slots, KG * BS, BS)
    up_partial = jnp.einsum(
        "tfkr,tfi->fkri", picked_up, up_grad, preferred_element_type=jnp.float32
    ).reshape(owned_slots, KG * BS, BS)
    down_partial = jnp.einsum(
        "tfkj,tfi->fkji", picked_grad, hidden, preferred_element_type=jnp.float32
    ).reshape(owned_slots, KH * BS, BS)
    tile_sums = lax.psum_scatter(
        jnp.concatenate([gate_partial, up_partial, down_partial], axis=0).astype(jnp.bfloat16),
        "row",
        scatter_dimension=1,
        tiled=True,
    )
    panel_sums = lax.psum_scatter(
        jnp.stack([partial_out, partial_in]).astype(jnp.bfloat16),
        "col",
        scatter_dimension=2,
        tiled=True,
    )
    return (
        panel_sums[0],
        panel_sums[1],
        tile_sums[:owned_slots],
        tile_sums[owned_slots : 2 * owned_slots],
        tile_sums[2 * owned_slots :],
    )


def solution(mesh):
    in_specs = (
        P("row", "col"),
        P("row", "col"),
        P("col", "row", None),
        P("col", "row", None),
        P("col", "row", None),
        P("col", None),
        P("col", None),
        P("col", None),
    )
    out_specs = (
        P("row", "col"),
        P("row", "col"),
        P("col", "row", None),
        P("col", "row", None),
        P("col", "row", None),
    )
    return jax.shard_map(shards, mesh=mesh, in_specs=in_specs, out_specs=out_specs, check_vma=False)
```

profile of v0, /device:TPU:2, one launch (start us, length us, event | category | flops | bytes accessed | tf_op | source)
XLA Modules:
  0.0 436.0 jit_solution(9459463797062491396)
XLA Ops:
  7.2 0.0 all-gather.3.cloned.1.call-start
  7.2 1.8 pad_maximum_fusion.3
  9.0 0.0 all-gather.3.cloned.1.call-update
  9.0 0.0 all-gather.5.cloned.1.call-start
  9.1 1.1 copy.50
  10.2 1.1 copy.51
  11.3 0.8 pad_maximum_fusion.2
  12.1 0.0 reduce-scatter.5.cloned.1.call-start
  12.2 0.8 reshape.183
  13.0 0.1 reshape.187
  13.0 0.1 reshape.180
  13.2 43.8 %all-gather.3.cloned.1.call-done = bf16[21,1024,128]{2,1,0:T(8,128)(2,1)} async-done(((bf16[21,64,128]{2,1,0:T(8,128)(2,1)}), bf16[21,1024,128]{2,1,0:T(8,128)(2,1)}) %all-gather.3.cloned.1.call-update) | async-done | bytes 5505040 | tf_op jit(solution)/shard_map/all_gather | solution.py:25
  57.1 4.9 %fusion.10 = (bf16[7,1024,128]{2,1,0:T(8,128)(2,1)}, bf16[7,1024,128]{2,1,0:T(8,128)(2,1)}, bf16[7,1024,128]{2,1,0:T(8,128)(2,1)S(1)}) fusion(bf16[21,1024,128]{2,1,0:T(8,128)(2,1)} %all-gather.3.cloned.1.call-done), kind=kLoop, calls=%fused_computation.48 | loop fusion | bytes 11010048 | tf_op jit(solution)/shard_map/slice | solution.py:29
  61.9 71.8 %all-gather.5.cloned.1.call-done = bf16[2,256,8192]{1,2,0:T(8,128)(2,1)} async-done(((bf16[2,256,512]{1,2,0:T(8,128)(2,1)}), bf16[2,256,8192]{1,2,0:T(8,128)(2,1)}) %all-gather.5.cloned.1.call-update) | async-done | bytes 8388624 | tf_op jit(solution)/shard_map/all_gather | solution.py:21
  133.7 5.7 %fusion.9 = (bf16[1,256,8192]{1,2,0:T(8,128)(2,1)}, bf16[1,256,8192]{1,2,0:T(8,128)(2,1)}) fusion(bf16[2,256,8192]{1,2,0:T(8,128)(2,1)} %all-gather.5.cloned.1.call-done), kind=kLoop, calls=%fused_computation.47 | loop fusion | bytes 16777216 | tf_op jit(solution)/shard_map/slice | solution.py:22
  139.4 6.4 %copy.52 = bf16[256,64,128]{2,0,1:T(8,128)(2,1)} copy(bf16[256,64,128]{0,2,1:T(8,128)(2,1)} %bitcast.106) | data formatting | bytes 8388608 | tf_op jit(solution)/shard_map/reshape;squeeze | solution.py:33
  145.9 6.4 %copy.59 = bf16[256,64,128]{2,0,1:T(8,128)(2,1)} copy(bf16[256,64,128]{0,2,1:T(8,128)(2,1)} %bitcast.105) | data formatting | bytes 8388608 | tf_op jit(solution)/shard_map/reshape;squeeze | solution.py:50
  152.2 5.1 %gather_fusion.1 = bf16[56,256,128]{2,1,0:T(8,128)(2,1)} fusion(bf16[256,64,128]{2,0,1:T(8,128)(2,1)} %copy.52, s32[1024]{0:T(1024)S(1)} %pad_clamp_fusion.1), kind=kCustom, calls=%fused_computation.1.clone | custom fusion | bytes 7340256 | tf_op jit(solution)/shard_map/jit(_take)/gather | solution.py:37
  157.3 5.1 %gather_fusion = bf16[56,256,128]{2,1,0:T(8,128)(2,1)} fusion(bf16[256,64,128]{2,0,1:T(8,128)(2,1)} %copy.52, s32[1024]{0:T(1024)S(1)} %pad_clamp_fusion.2), kind=kCustom, calls=%fused_computation.clone | custom fusion | bytes 7340256 | tf_op jit(solution)/shard_map/jit(_take)/gather | solution.py:34
  162.4 2.6 broadcast_select_fusion.1
  165.0 1.8 copy-done
  166.8 2.3 convolution_bitcast_fusion.1
  169.0 5.1 %gather_fusion.2 = bf16[56,256,128]{2,1,0:T(8,128)(2,1)} fusion(bf16[256,64,128]{2,0,1:T(8,128)(2,1)} %copy.59, s32[1024]{0:T(1024)S(1)} %pad_clamp_fusion), kind=kCustom, calls=%fused_computation.2.clone | custom fusion | bytes 7340256 | tf_op jit(solution)/shard_map/jit(_take)/gather | solution.py:51
  174.1 2.4 broadcast_select_fusion
  176.6 1.4 convolution_bitcast_fusion
  177.9 0.7 copy-done.3
  178.6 0.4 broadcast_select_fusion.2
  179.0 1.1 copy-done.4
  180.1 0.2 copy-done.5
  180.3 1.6 fusion.1
  181.9 1.4 convolution_convert_fusion.2
  183.3 0.7 copy-done.1
  184.0 1.4 convolution_convert_fusion.1
  185.3 1.4 convolution_convert_fusion
  186.7 2.9 pad_maximum_fusion.1
  189.6 0.0 reduce-scatter.5.cloned.1.call-update
  189.6 0.2 reduce-scatter.3.cloned.1.call-start
  189.9 0.4 copy-done.6
  190.3 0.1 reshape.190
  190.4 0.1 reshape.186
  190.5 0.1 reshape.177
  190.6 5.6 %fusion.13 = f32[7,8,128,256]{3,2,1,0:T(8,128)} fusion(bf16[7,8,128,128]{3,2,1,0:T(8,128)(2,1)} %bitcast.110, bf16[256,7,128,1]{0,2,3,1:T(8,128)(2,1)S(1)} %get-tuple-element.23), kind=kOutput, calls=%fused_computation.51 | convolution fusion | flops 469762048 | bytes 9633792 | tf_op jit(solution)/shard_map/tfi,fkri->tfkr/dot_general | solution.py:64
  196.2 8.4 %copy.64 = f32[256,56,128]{2,0,1:T(8,128)} copy(f32[256,56,128]{0,2,1:T(8,128)} %bitcast.98) | data formatting | bytes 14680064 | tf_op jit(solution)/shard_map/reshape | solution.py:16
  204.6 5.6 %fusion.4 = f32[7,8,128,256]{3,2,1,0:T(8,128)} fusion(bf16[7,8,128,128]{3,2,1,0:T(8,128)(2,1)} %bitcast.114, bf16[256,7,128]{0,2,1:T(8,128)(2,1)S(1)} %get-tuple-element.22), kind=kOutput, calls=%fused_computation.27 | convolution fusion | flops 469762048 | bytes 9633792 | tf_op jit(solution)/shard_map/tfi,fkri->tfkr/dot_general | solution.py:61
  210.2 8.4 %copy.62 = f32[256,56,128]{2,0,1:T(8,128)} copy(f32[256,56,128]{0,2,1:T(8,128)} %bitcast.99) | data formatting | bytes 14680064 | tf_op jit(solution)/shard_map/reshape | solution.py:16
  218.6 4.3 broadcast.57.clone.1
  222.8 19.0 %scatter_fusion.2 = f32[256,64,128]{2,0,1:T(8,128)} fusion(f32[256,64,128]{2,0,1:T(8,128)} %broadcast.57.clone.1, s32[56]{0:T(128)S(1)} %fusion.8, f32[56,256,128]{2,1,0:T(8,128)} %bitcast.101), kind=kCustom, calls=%fused_computation.5 | custom fusion | flops 1835008 | bytes 22020320 | tf_op jit(solution)/shard_map/scatter-add | solution.py:16
  241.8 4.2 broadcast.57.clone
  246.1 19.1 %scatter_fusion.1 = f32[256,64,128]{2,0,1:T(8,128)} fusion(f32[256,64,128]{2,0,1:T(8,128)} %broadcast.57.clone, s32[56]{0:T(128)S(1)} %fusion.7, f32[56,256,128]{2,1,0:T(8,128)} %bitcast.102), kind=kCustom, calls=%fused_computation.4 | custom fusion | flops 1835008 | bytes 22020320 | tf_op jit(solution)/shard_map/scatter-add | solution.py:16
  265.2 9.5 %add_convert_fusion = bf16[256,64,128]{2,0,1:T(8,128)(2,1)} fusion(f32[256,64,128]{2,0,1:T(8,128)} %scatter_fusion.1, f32[256,64,128]{2,0,1:T(8,128)} %scatter_fusion.2), kind=kLoop, calls=%fused_computation.7 | loop fusion | flops 4194304 | bytes 20971520 | tf_op jit(solution)/shard_map/convert.8
  274.7 6.4 %copy.65 = bf16[256,64,128]{0,2,1:T(8,128)(2,1)} copy(bf16[256,64,128]{2,0,1:T(8,128)(2,1)} %add_convert_fusion) | data formatting | bytes 8388608 | tf_op jit(solution)/shard_map/convert.8
  281.1 4.0 fusion.12
  285.2 8.3 %copy.57 = f32[256,56,128]{2,0,1:T(8,128)} copy(f32[256,56,128]{0,2,1:T(8,128)} %bitcast.100) | data formatting | bytes 14680064 | tf_op jit(solution)/shard_map/reshape | solution.py:16
  293.5 4.2 broadcast.57.clone.2
  297.7 18.8 %scatter_fusion = f32[256,64,128]{2,0,1:T(8,128)} fusion(f32[256,64,128]{2,0,1:T(8,128)} %broadcast.57.clone.2, s32[56]{0:T(128)S(1)} %fusion.6, f32[56,256,128]{2,1,0:T(8,128)} %bitcast.103), kind=kCustom, calls=%fused_computation.3 | custom fusion | flops 1835008 | bytes 22020320 | tf_op jit(solution)/shard_map/scatter-add | solution.py:16
  316.6 6.1 %convert.20 = bf16[256,64,128]{2,0,1:T(8,128)(2,1)} convert(f32[256,64,128]{2,0,1:T(8,128)} %scatter_fusion) | non-fusion elementwise | flops 2097152 | bytes 12582912 | tf_op jit(solution)/shard_map/convert.9
  322.7 6.4 %copy.58 = bf16[256,64,128]{0,2,1:T(8,128)(2,1)} copy(bf16[256,64,128]{2,0,1:T(8,128)(2,1)} %convert.20) | data formatting | bytes 8388608 | tf_op jit(solution)/shard_map/convert.9
  329.0 7.4 %pad_maximum_fusion = bf16[2,256,8192]{1,2,0:T(8,128)(2,1)} fusion(bf16[1,256,8192]{1,2,0:T(8,128)(2,1)} %bitcast.104, bf16[1,256,8192]{1,2,0:T(8,128)(2,1)} %bitcast.107), kind=kLoop, calls=%fused_computation.6 | loop fusion | flops 4194304 | bytes 16777216 | tf_op jit(solution)/shard_map/stack | solution.py:82
  336.5 0.0 reduce-scatter.5.cloned.1.call-done
  336.5 1.7 fusion.11
  338.3 88.4 %reduce-scatter.3.cloned.1.call-done = bf16[2,256,512]{1,2,0:T(8,128)(2,1)} async-done(((bf16[2,256,8192]{1,2,0:T(8,128)(2,1)}), bf16[2,256,512]{1,2,0:T(8,128)(2,1)}) %reduce-scatter.3.cloned.1.call-update) | async-done | bytes 524304 | tf_op jit(solution)/shard_map/reduce_scatter | solution.py:81
  426.7 1.1 slice_bitcast_fusion
  427.7 0.8 copy.72
  428.6 0.8 copy.73
  (26 shorter events, 0.1 us)
Async XLA Ops:
  7.2 5.8 %copy-start.8 = (s32[7,8]{1,0:T(8,128)S(1)}, s32[7,8]{1,0:T(8,128)}, u32[]{:S(2)}) copy-start(s32[7,8]{1,0:T(8,128)} %param.17) | copy-start | bytes 676
  7.2 5.9 %copy-start.7 = (s32[7,8]{1,0:T(8,128)S(1)}, s32[7,8]{1,0:T(8,128)}, u32[]{:S(2)}) copy-start(s32[7,8]{1,0:T(8,128)} %param.15) | copy-start | bytes 676
  7.2 49.9 %all-gather.3.cloned.1.call-start = ((), (), s32[]{:S(2)}) async-start(), calls=%async_computation.2 | async-start | bytes 5849088 | tf_op jit(solution)/shard_map/all_gather | solution.py:25
  9.0 124.7 %all-gather.5.cloned.1.call-start = ((), (), s32[]{:S(2)}) async-start(), calls=%async_computation.3 | async-start | bytes 8912896 | tf_op jit(solution)/shard_map/all_gather | solution.py:21
  12.1 324.4 %reduce-scatter.5.cloned.1.call-start = ((), (), s32[]{:S(2)}) async-start(), calls=%async_computation.5 | async-start | bytes 5849088 | tf_op jit(solution)/shard_map/reduce_scatter | solution.py:75
  162.4 4.4 %copy-start.2 = (bf16[7,1024,128]{2,1,0:T(8,128)(2,1)S(1)}, bf16[7,1024,128]{2,1,0:T(8,128)(2,1)}, u32[]{:S(2)}) copy-start(bf16[7,1024,128]{2,1,0:T(8,128)(2,1)} %get-tuple-element.18) | copy-start | bytes 5505028
  164.9 1.8 copy-start
  176.5 2.0 copy-start.3
  178.6 1.5 copy-start.4
  178.6 1.7 copy-start.5
  181.9 2.0 copy-start.1
  189.6 0.7 copy-start.6
  189.6 237.0 %reduce-scatter.3.cloned.1.call-start = ((), (), s32[]{:S(2)}) async-start(), calls=%async_computation.4 | async-start | bytes 8912896 | tf_op jit(solution)/shard_map/reduce_scatter | solution.py:81
Sparse Core Ops, SparseCore 0:
  9.9 47.1 all-gather.2
  59.6 74.1 all-gather.4
  189.8 64.9 reduce-scatter.4
  336.6 89.9 reduce-scatter.2
where the time goes:
time: 438 us; the launch traced here: 436 us
  waiting for transfers between devices  204 us (47%)
  local copies, waits for them, and re-layouts  102 us (23%)
  other arithmetic  91 us (21%)
  matrix products  24.6 us (6%)
  between operations  14 us (3%)
    reduce_scatter x1, waiting for transfers between devices, shards(): lax.psum_scatter(jnp.stack([partial_out, partial_in]).astype(jnp.bfloat16...  88.4 us
    all_gather x1, waiting for transfers between devices, shards(): lax.all_gather(jnp.stack([tokens, out_grad]), 'col', axis=2, tiled=True)  71.8 us
    scatter-add x3, other arithmetic, spread(): zero_block.at[:, block_lists.reshape(-1)]  56.9 us
    all_gather x1, waiting for transfers between devices, shards(): lax.all_gather(jnp.concatenate([gate_weight, up_weight, down_weight], axi...  43.8 us
    another operation x5, local copies, waits for them, and re-layouts  25.5 us
    reshape x3, local copies, waits for them, and re-layouts, spread(): contrib.reshape(rows_here, -1, BS)  25.1 us
    another operation x2, other arithmetic  15.6 us
  transfers between devices with their start and end apart: 4, of which 3 were waited for; matrix products, arithmetic and copies ran while one was open for 36% of the time, Pallas kernels for 0%

commit v1 on v0

--- a/solution.py
+++ b/solution.py
@@ -18,7 +18,9 @@
 
 
 def shards(tokens, out_grad, gate_weight, up_weight, down_weight, gate_rows, up_rows, down_columns):
-    panels = lax.all_gather(jnp.stack([tokens, out_grad]), "col", axis=2, tiled=True)
+    x = jnp.stack([tokens, out_grad])
+    copies = jnp.concatenate([x] * lax.axis_size("col"), axis=2)
+    panels = lax.all_to_all(copies, "col", 2, 2, tiled=True)
     panel_in, panel_grad = (panels[0], panels[1])
     rows_here = panel_in.shape[0]
     owned_slots = gate_weight.shape[0]

time: 438 us -> 537 us (1.23)
  local copies, waits for them, and re-layouts: 102 us -> 137 us
  waiting for transfers between devices: 204 us -> 238 us
  other arithmetic: 91 us -> 113 us
  starting transfers between devices: 0.34 us -> 7.74 us
    all_to_all x0 -> x1, waiting for transfers between devices: none -> 104 us  [shards(): panels = lax.all_to_all(copies, 'col', 2, 2, tiled=True)]
    all_gather x1 -> x0, waiting for transfers between devices: 71.8 us -> none  [shards(): lax.all_gather(jnp.stack([tokens, out_grad]), 'col', axis=2, tiled=True)]
    reduce_scatter x1, waiting for transfers between devices: 88.4 us -> 135 us  [shards(): lax.psum_scatter(jnp.stack([partial_out, partial_in]).astype(jnp.bfloat16...]
    all_gather x1, waiting for transfers between devices: 43.8 us -> 0.01 us  [shards(): lax.all_gather(jnp.concatenate([gate_weight, up_weight, down_weight], axi...]
    concatenate x0 -> x1, local copies, waits for them, and re-layouts: none -> 21 us  [shards(): copies = jnp.concatenate([x] * lax.axis_size('col'), axis=2)]
    unnamed x0 -> x15, other arithmetic: none -> 19.3 us
    slice x1, local copies, waits for them, and re-layouts: 5.71 us -> 17.2 us  [shards(): panel_in, panel_grad = (panels[0], panels[1])]
    all_to_all x0 -> x1, starting transfers between devices: none -> 7.62 us  [shards(): panels = lax.all_to_all(copies, 'col', 2, 2, tiled=True)]
  transfers between devices with their start and end apart: 4 -> 4, of which waited for: 3 -> 2; matrix products, arithmetic and copies ran while one was open for 36% -> 40% of each run, Pallas kernels for 0% -> 0%
where the time goes in v1:
time: 537 us; the launch traced here: 535 us
  waiting for transfers between devices  238 us (44%)
  local copies, waits for them, and re-layouts  137 us (26%)
  other arithmetic  113 us (21%)
  matrix products  23.7 us (4%)
  between operations  14 us (3%)
  starting transfers between devices  7.74 us (1%)
    reduce_scatter x1, waiting for transfers between devices, shards(): lax.psum_scatter(jnp.stack([partial_out, partial_in]).astype(jnp.bfloat16...  135 us
    all_to_all x1, waiting for transfers between devices, shards(): panels = lax.all_to_all(copies, 'col', 2, 2, tiled=True)  104 us
    scatter-add x3, other arithmetic, spread(): zero_block.at[:, block_lists.reshape(-1)]  57.2 us
    another operation x5, local copies, waits for them, and re-layouts  25.5 us
    reshape x3, local copies, waits for them, and re-layouts, spread(): contrib.reshape(rows_here, -1, BS)  25.1 us
    concatenate x1, local copies, waits for them, and re-layouts, shards(): copies = jnp.concatenate([x] * lax.axis_size('col'), axis=2)  21 us
    unnamed x15, other arithmetic  19.3 us
    slice x1, local copies, waits for them, and re-layouts, shards(): panel_in, panel_grad = (panels[0], panels[1])  17.2 us
  transfers between devices with their start and end apart: 4, of which 2 were waited for; matrix products, arithmetic and copies ran while one was open for 40% of the time, Pallas kernels for 0%

profile of v1, /device:TPU:2, one launch (start us, length us, event | category | flops | bytes accessed | tf_op | source)
XLA Modules:
  0.0 534.5 jit_solution(9399905480936158432)
XLA Ops:
  7.2 1.9 constant_dynamic-update-slice_fusion.15
  9.1 1.9 constant_dynamic-update-slice_fusion.14
  11.0 1.9 constant_dynamic-update-slice_fusion.13
  12.9 1.9 constant_dynamic-update-slice_fusion.12
  14.8 1.9 constant_dynamic-update-slice_fusion.11
  16.7 1.9 constant_dynamic-update-slice_fusion.10
  18.6 0.9 constant_dynamic-update-slice_fusion.9
  19.5 0.9 constant_dynamic-update-slice_fusion.8
  20.4 0.9 constant_dynamic-update-slice_fusion.7
  21.2 0.9 constant_dynamic-update-slice_fusion.6
  22.1 0.9 constant_dynamic-update-slice_fusion.5
  23.0 0.9 constant_dynamic-update-slice_fusion.4
  23.8 0.9 constant_dynamic-update-slice_fusion.3
  24.7 0.9 constant_dynamic-update-slice_fusion.2
  25.6 0.9 constant_dynamic-update-slice_fusion.1
  26.5 0.9 constant_dynamic-update-slice_fusion
  27.5 21.0 %copy.100 = bf16[2,256,8192]{1,0,2:T(2,128)(2,1)} copy(bf16[2,256,8192]{2,1,0:T(8,128)(2,1)} %constant_dynamic-update-slice_fusion) | data formatting | bytes 16777216 | tf_op jit(solution)/shard_map/concatenate | solution.py:22
  48.5 7.6 %all-to-all-start = ((bf16[2,256,8192]{1,0,2:T(2,128)(2,1)}), bf16[2,256,8192]{1,0,2:T(2,128)(2,1)}, u32[]{:S(2)}, u32[]{:S(2)}) async-start(bf16[2,256,8192]{1,0,2:T(2,128)(2,1)} %copy.100), calls=%async_computation | async-start | bytes 16777216 | tf_op jit(solution)/shard_map/all_to_all | solution.py:23
  56.2 0.8 pad_maximum_fusion.3
  57.4 103.5 %all-to-all-done = bf16[2,256,8192]{1,0,2:T(2,128)(2,1)} async-done(((bf16[2,256,8192]{1,0,2:T(2,128)(2,1)}), bf16[2,256,8192]{1,0,2:T(2,128)(2,1)}, u32[]{:S(2)}, u32[]{:S(2)}) %all-to-all-start) | async-done | bytes 8388640 | tf_op jit(solution)/shard_map/all_to_all | solution.py:23
  160.9 17.2 %fusion.9 = (bf16[1,256,8192]{1,0,2:T(2,128)(2,1)S(1)}, bf16[1,256,8192]{1,0,2:T(2,128)(2,1)}) fusion(bf16[2,256,8192]{1,0,2:T(2,128)(2,1)} %all-to-all-done), kind=kLoop, calls=%fused_computation.63 | loop fusion | bytes 16777216 | tf_op jit(solution)/shard_map/slice | solution.py:24
  178.2 2.9 copy.153
  181.0 6.4 %copy.110 = bf16[256,64,128]{2,0,1:T(8,128)(2,1)} copy(bf16[256,64,128]{0,2,1:T(8,128)(2,1)} %bitcast.136) | data formatting | bytes 8388608 | tf_op jit(solution)/shard_map/reshape;squeeze | solution.py:52
  187.4 6.1 %copy.152 = bf16[1,256,8192]{1,2,0:T(8,128)(2,1)} copy(bf16[1,256,8192]{1,0,2:T(2,128)(2,1)} %get-tuple-element.27) | data formatting | bytes 8388608
  193.6 6.4 %copy.102 = bf16[256,64,128]{2,0,1:T(8,128)(2,1)} copy(bf16[256,64,128]{0,2,1:T(8,128)(2,1)} %bitcast.137) | data formatting | bytes 8388608 | tf_op jit(solution)/shard_map/reshape;squeeze | solution.py:35
  200.0 5.0 gather_fusion.1
  205.0 5.1 gather_fusion
  210.1 5.1 gather_fusion.2
  215.2 4.4 broadcast_select_fusion
  219.6 2.3 broadcast_select_fusion.1
  221.8 1.1 copy-done.6
  222.9 2.2 broadcast_select_fusion.2
  225.2 3.2 fusion.10
  228.4 0.4 copy-done.2
  228.9 1.4 convolution_bitcast_fusion
  230.2 1.7 copy-done.3
  231.9 1.3 convolution_bitcast_fusion.1
  233.3 1.6 fusion.1
  234.9 1.4 convolution_convert_fusion.2
  236.3 1.4 convolution_convert_fusion.1
  237.6 1.4 convolution_convert_fusion
  239.0 2.9 pad_maximum_fusion.1
  242.2 5.6 %fusion.13 = f32[7,8,128,256]{3,2,1,0:T(8,128)} fusion(bf16[7,8,128,128]{3,2,1,0:T(8,128)(2,1)} %bitcast.143, bf16[256,7,128,1]{0,2,3,1:T(8,128)(2,1)S(1)} %get-tuple-element.33), kind=kOutput, calls=%fused_computation.67 | convolution fusion | flops 469762048 | bytes 9633792 | tf_op jit(solution)/shard_map/tfi,fkri->tfkr/dot_general | solution.py:66
  247.8 8.4 %copy.115 = f32[256,56,128]{2,0,1:T(8,128)} copy(f32[256,56,128]{0,2,1:T(8,128)} %bitcast.130) | data formatting | bytes 14680064 | tf_op jit(solution)/shard_map/reshape | solution.py:16
  256.2 5.6 %fusion.4 = f32[7,8,128,256]{3,2,1,0:T(8,128)} fusion(bf16[7,8,128,128]{3,2,1,0:T(8,128)(2,1)} %bitcast.147, bf16[256,7,128]{0,2,1:T(8,128)(2,1)S(1)} %get-tuple-element.32), kind=kOutput, calls=%fused_computation.27 | convolution fusion | flops 469762048 | bytes 9633792 | tf_op jit(solution)/shard_map/tfi,fkri->tfkr/dot_general | solution.py:63
  261.8 8.4 %copy.113 = f32[256,56,128]{2,0,1:T(8,128)} copy(f32[256,56,128]{0,2,1:T(8,128)} %bitcast.131) | data formatting | bytes 14680064 | tf_op jit(solution)/shard_map/reshape | solution.py:16
  270.2 4.3 broadcast.57.clone.1
  274.4 18.9 %scatter_fusion.2 = f32[256,64,128]{2,0,1:T(8,128)} fusion(f32[256,64,128]{2,0,1:T(8,128)} %broadcast.57.clone.1, s32[56]{0:T(128)S(1)} %fusion.8, f32[56,256,128]{2,1,0:T(8,128)} %bitcast.133), kind=kCustom, calls=%fused_computation.5 | custom fusion | flops 1835008 | bytes 22020320 | tf_op jit(solution)/shard_map/scatter-add | solution.py:16
  293.3 4.3 broadcast.57.clone
  297.6 19.3 %scatter_fusion.1 = f32[256,64,128]{2,0,1:T(8,128)} fusion(f32[256,64,128]{2,0,1:T(8,128)} %broadcast.57.clone, s32[56]{0:T(128)S(1)} %fusion.7, f32[56,256,128]{2,1,0:T(8,128)} %bitcast.134), kind=kCustom, calls=%fused_computation.4 | custom fusion | flops 1835008 | bytes 22020320 | tf_op jit(solution)/shard_map/scatter-add | solution.py:16
  316.8 9.8 %add_convert_fusion = bf16[256,64,128]{2,0,1:T(8,128)(2,1)} fusion(f32[256,64,128]{2,0,1:T(8,128)} %scatter_fusion.1, f32[256,64,128]{2,0,1:T(8,128)} %scatter_fusion.2), kind=kLoop, calls=%fused_computation.7 | loop fusion | flops 4194304 | bytes 20971520 | tf_op jit(solution)/shard_map/convert.8
  326.7 6.4 %copy.116 = bf16[256,64,128]{0,2,1:T(8,128)(2,1)} copy(bf16[256,64,128]{2,0,1:T(8,128)(2,1)} %add_convert_fusion) | data formatting | bytes 8388608 | tf_op jit(solution)/shard_map/convert.8
  333.1 4.0 fusion.12
  337.1 8.4 %copy.107 = f32[256,56,128]{2,0,1:T(8,128)} copy(f32[256,56,128]{0,2,1:T(8,128)} %bitcast.132) | data formatting | bytes 14680064 | tf_op jit(solution)/shard_map/reshape | solution.py:16
  345.5 4.3 broadcast.57.clone.2
  349.7 19.0 %scatter_fusion = f32[256,64,128]{2,0,1:T(8,128)} fusion(f32[256,64,128]{2,0,1:T(8,128)} %broadcast.57.clone.2, s32[56]{0:T(128)S(1)} %fusion.6, f32[56,256,128]{2,1,0:T(8,128)} %bitcast.135), kind=kCustom, calls=%fused_computation.3 | custom fusion | flops 1835008 | bytes 22020320 | tf_op jit(solution)/shard_map/scatter-add | solution.py:16
  368.7 6.1 %convert.20 = bf16[256,64,128]{2,0,1:T(8,128)(2,1)} convert(f32[256,64,128]{2,0,1:T(8,128)} %scatter_fusion) | non-fusion elementwise | flops 2097152 | bytes 12582912 | tf_op jit(solution)/shard_map/convert.9
  374.8 6.4 %copy.108 = bf16[256,64,128]{0,2,1:T(8,128)(2,1)} copy(bf16[256,64,128]{2,0,1:T(8,128)(2,1)} %convert.20) | data formatting | bytes 8388608 | tf_op jit(solution)/shard_map/convert.9
  381.2 7.5 %pad_maximum_fusion = bf16[2,256,8192]{1,2,0:T(8,128)(2,1)} fusion(bf16[1,256,8192]{1,2,0:T(8,128)(2,1)} %bitcast.138, bf16[1,256,8192]{1,2,0:T(8,128)(2,1)} %bitcast.139), kind=kLoop, calls=%fused_computation.6 | loop fusion | flops 4194304 | bytes 16777216 | tf_op jit(solution)/shard_map/stack | solution.py:84
  388.7 1.7 fusion.11
  390.5 134.8 %reduce-scatter.3.cloned.1.call-done = bf16[2,256,512]{1,2,0:T(8,128)(2,1)} async-done(((bf16[2,256,8192]{1,2,0:T(8,128)(2,1)}), bf16[2,256,512]{1,2,0:T(8,128)(2,1)}) %reduce-scatter.3.cloned.1.call-update) | async-done | bytes 524304 | tf_op jit(solution)/shard_map/reduce_scatter | solution.py:83
  525.2 1.1 slice_bitcast_fusion
  526.3 0.8 copy.123
  527.2 0.8 copy.124
  (52 shorter events, 0.8 us)
Async XLA Ops:
  7.2 11.5 %copy-start.1 = (bf16[256,512]{1,0:T(8,128)(2,1)S(1)}, bf16[256,512]{1,0:T(8,128)(2,1)}, u32[]{:S(2)}) copy-start(bf16[256,512]{1,0:T(8,128)(2,1)} %param.10) | copy-start | bytes 786436
  7.2 11.4 %copy-start = (bf16[256,512]{1,0:T(8,128)(2,1)S(1)}, bf16[256,512]{1,0:T(8,128)(2,1)}, u32[]{:S(2)}) copy-start(bf16[256,512]{1,0:T(8,128)(2,1)} %param.11) | copy-start | bytes 786436
  48.5 7.7 %copy-start.9 = (bf16[7,64,128]{2,1,0:T(8,128)(2,1)S(1)}, bf16[7,64,128]{2,1,0:T(8,128)(2,1)}, u32[]{:S(2)}) copy-start(bf16[7,64,128]{2,1,0:T(8,128)(2,1)} %param.14) | copy-start | bytes 344068
  48.5 7.7 %copy-start.10 = (bf16[7,64,128]{2,1,0:T(8,128)(2,1)S(1)}, bf16[7,64,128]{2,1,0:T(8,128)(2,1)}, u32[]{:S(2)}) copy-start(bf16[7,64,128]{2,1,0:T(8,128)(2,1)} %param.13) | copy-start | bytes 344068
  48.5 7.7 %copy-start.11 = (bf16[7,64,128]{2,1,0:T(8,128)(2,1)S(1)}, bf16[7,64,128]{2,1,0:T(8,128)(2,1)}, u32[]{:S(2)}) copy-start(bf16[7,64,128]{2,1,0:T(8,128)(2,1)} %param.12) | copy-start | bytes 344068
  48.5 8.6 %copy-start.14 = (s32[7,8]{1,0:T(8,128)S(1)}, s32[7,8]{1,0:T(8,128)}, u32[]{:S(2)}) copy-start(s32[7,8]{1,0:T(8,128)} %param.17) | copy-start | bytes 676
  48.5 8.7 %copy-start.12 = (s32[7,8]{1,0:T(8,128)S(1)}, s32[7,8]{1,0:T(8,128)}, u32[]{:S(2)}) copy-start(s32[7,8]{1,0:T(8,128)} %param.16) | copy-start | bytes 676
  48.5 8.7 %copy-start.13 = (s32[7,8]{1,0:T(8,128)S(1)}, s32[7,8]{1,0:T(8,128)}, u32[]{:S(2)}) copy-start(s32[7,8]{1,0:T(8,128)} %param.15) | copy-start | bytes 676
  48.5 112.4 %all-to-all-start = ((bf16[2,256,8192]{1,0,2:T(2,128)(2,1)}), bf16[2,256,8192]{1,0,2:T(2,128)(2,1)}, u32[]{:S(2)}, u32[]{:S(2)}) async-start(bf16[2,256,8192]{1,0,2:T(2,128)(2,1)} %copy.100), calls=%async_computation | async-start | bytes 16777216 | tf_op jit(solution)/shard_map/all_to_all | solution.py:23
  56.1 169.1 %all-gather.2.cloned.1.call-start = ((), (), s32[]{:S(2)}) async-start(), calls=%async_computation.3 | async-start | bytes 5849088 | tf_op jit(solution)/shard_map/all_gather | solution.py:27
  57.0 331.7 %reduce-scatter.5.cloned.1.call-start = ((), (), s32[]{:S(2)}) async-start(), calls=%async_computation.5 | async-start | bytes 5849088 | tf_op jit(solution)/shard_map/reduce_scatter | solution.py:77
  215.2 4.4 copy-start.7
  219.6 3.4 copy-start.6
  225.2 3.7 copy-start.2
  228.4 4.8 copy-start.4
  228.4 4.8 copy-start.8
  228.4 3.5 copy-start.3
  228.9 4.4 copy-start.5
  241.9 283.3 %reduce-scatter.3.cloned.1.call-start = ((), (), s32[]{:S(2)}) async-start(), calls=%async_computation.4 | async-start | bytes 8912896 | tf_op jit(solution)/shard_map/reduce_scatter | solution.py:83
Sparse Core Ops, SparseCore 0:
  58.8 46.8 all-gather.1
  242.0 111.8 reduce-scatter.4
  388.8 136.3 reduce-scatter.2
